TPU v7x, 32 devices: a whole 2x2x4 slice. The times are simulated.
32 devices in a mesh: dp: 8 (over z, x), tensor: 4 (over y, core).
Axes of the slice: x: 2, y: 2, z: 4, core: 2. Of those that a mesh axis runs over, the one named last changes fastest.
Arguments:
- context: bfloat16 [2, 8192, 3072], P(None, 'dp', 'tensor'), may hold values from -6 to 6
- out_grad: bfloat16 [2, 8192, 3072], P(None, ('dp', 'tensor')), may hold values from -0.1875 to 0.1875
- error_in: bfloat16 [2, 24576, 3072], P(None, 'dp', 'tensor'), may hold values from -6 to 6
- right_init: float32 [2, 64, 3072], P(None, None, 'tensor'), may hold values from -6 to 6
Outputs:
- summed_update: bfloat16 [2, 3072, 3072], P(None, 'dp', 'tensor')
- error_out: bfloat16 [2, 24576, 3072], P(None, 'dp', 'tensor')
All inputs are finite; a program needn't handle non-finite values.
Results may differ from a plain program's by a relative error of at most 0.015.
Values may be sent and summed in bfloat16 or wider, within the bound.
A program may use at most 128 MiB of HBM per device.

v0:
```python
import jax
import jax.numpy as jnp
from jax import lax
from jax.sharding import PartitionSpec as P


def solve_rows(gram_matrix, left_factor):
    ridge_term = 1e-06 * jnp.mean(jnp.diagonal(gram_matrix, axis1=1, axis2=2), axis=1)
    eye_matrix = jnp.eye(gram_matrix.shape[1], dtype=gram_matrix.dtype)
    gram_matrix = gram_matrix + ridge_term[:, None, None] * eye_matrix
    factor_low = jnp.linalg.cholesky(gram_matrix)

    def one_solve(low_part, rhs_part):
        return jax.scipy.linalg.solve_triangular(low_part, rhs_part, lower=True)

    return jax.vmap(one_solve)(factor_low, left_factor)


def gram_of(left_factor):
    return jnp.einsum("lrd,lsd->lrs", left_factor, left_factor, precision=lax.Precision.HIGHEST)


def compress(context, out_grad, error_in, right_init):
    out_width = out_grad.shape[2]
    moment = jnp.einsum(
        "ltd,lte->lde",
        lax.all_gather(out_grad, "tensor", axis=1, tiled=True),
        context,
        preferred_element_type=jnp.float32,
    )
    moment = moment + error_in.astype(jnp.float32)
    left_factor = jnp.einsum("lre,lde->lrd", right_init, moment, precision=lax.Precision.HIGHEST)
    left_part = lax.psum_scatter(left_factor, "tensor", scatter_dimension=2, tiled=True)
    left_part = lax.psum(left_part, "dp")
    gram_matrix = lax.psum(gram_of(left_part), "tensor")
    ortho_part = solve_rows(gram_matrix, left_part)
    ortho_basis = lax.all_gather(ortho_part, "tensor", axis=2, tiled=True)
    right_terms = jnp.einsum("lrd,lde->lre", ortho_basis, moment, precision=lax.Precision.HIGHEST)
    right_factor = lax.psum(right_terms.astype(jnp.bfloat16), "dp").astype(jnp.float32)
    replicas = lax.axis_size("dp")
    row_share = out_width // replicas
    own_basis = lax.dynamic_slice_in_dim(
        ortho_basis, lax.axis_index("dp") * row_share, row_share, 2
    )
    summed = jnp.einsum("lrd,lre->lde", own_basis, right_factor, precision=lax.Precision.HIGHEST)
    mean_part = jnp.einsum(
        "lrd,lre->lde", ortho_basis, right_factor / replicas, precision=lax.Precision.HIGHEST
    )
    new_error = (moment - mean_part).astype(jnp.bfloat16)
    return (summed.astype(jnp.bfloat16), new_error)


def body(context, out_grad, error_in, right_init):
    return compress(context, out_grad, error_in, right_init)


def solution(mesh):
    return jax.shard_map(
        body,
        mesh=mesh,
        in_specs=(
            P(None, "dp", "tensor"),
            P(None, ("dp", "tensor"), None),
            P(None, "dp", "tensor"),
            P(None, None, "tensor"),
        ),
        out_specs=(P(None, "dp", "tensor"), P(None, "dp", "tensor")),
        check_vma=False,
    )
```

profile of v0, /device:TPU:0, one launch (start us, length us, event | category | flops | bytes accessed | tf_op | source)
XLA Modules:
  0.0 419.1 jit_solution(9212171889300298580)
XLA Ops:
  7.2 0.0 copy-start
  7.2 0.0 all-gather.3.cloned.1.call-start
  7.2 4.8 %copy.12 = bf16[2,256,3072]{1,2,0:T(8,128)(2,1)} copy(bf16[2,256,3072]{2,1,0:T(8,128)(2,1)} %param.5) | data formatting | bytes 6291456 | tf_op args[1]
  12.0 0.0 all-gather.3.cloned.1.call-update
  12.0 0.0 copy-start.4
  12.0 0.0 reduce-scatter.2.cloned.1.call-start
  12.1 86.6 %all-gather.3.cloned.1.call-done = bf16[2,1024,3072]{1,2,0:T(8,128)(2,1)} async-done(((bf16[2,256,3072]{1,2,0:T(8,128)(2,1)}), bf16[2,1024,3072]{1,2,0:T(8,128)(2,1)}) %all-gather.3.cloned.1.call-update) | async-done | bytes 12582928 | tf_op jit(solution)/shard_map/all_gather | solution.py:27
  98.7 0.0 copy-done
  98.7 19.3 %convert_add_fusion = f32[2,3072,768]{2,1,0:T(8,128)} fusion(bf16[2,3072,768]{2,1,0:T(8,128)(2,1)} %param.6, bf16[2,1024,3072]{1,2,0:T(8,128)(2,1)} %all-gather.3.cloned.1.call-done, bf16[2,1024,768]{2,1,0:T(8,128)(2,1)S(1)} %copy-done), kind=kOutput, calls=%fused_computation.2 | convolution fusion | flops 9673113600 | bytes 44040192 | tf_op jit(solution)/shard_map/ltd,lte->lde/dot_general | solution.py:25
  118.0 0.0 copy-done.4
  118.0 22.5 %convolution_bitcast_fusion = f32[2,64,3072]{2,1,0:T(8,128)} fusion(f32[2,3072,768]{2,1,0:T(8,128)} %convert_add_fusion, f32[2,64,768]{2,1,0:T(8,128)S(1)} %copy-done.4), kind=kOutput, calls=%fused_computation.3 | convolution fusion | flops 3623878656 | bytes 20840448 | tf_op jit(solution)/shard_map/lre,lde->lrd/dot_general | solution.py:32
  140.5 0.0 reduce-scatter.2.cloned.1.call-update
  140.5 0.0 all-reduce.3.cloned.1.call-start
  140.5 28.1 %reduce-scatter.2.cloned.1.call-done = f32[2,64,768]{2,1,0:T(8,128)} async-done(((f32[2,64,3072]{2,1,0:T(8,128)}), f32[2,64,768]{2,1,0:T(8,128)}) %reduce-scatter.2.cloned.1.call-update) | async-done | bytes 393232 | tf_op jit(solution)/shard_map/reduce_scatter | solution.py:33
  168.6 0.0 all-reduce.3.cloned.1.call-update
  168.7 0.0 all-gather.5.cloned.1.call-start
  168.7 0.1 copy.15
  168.9 75.0 %all-reduce.3.cloned.1.call-done = f32[2,64,768]{2,1,0:T(8,128)} async-done(((f32[2,64,768]{2,1,0:T(8,128)}), f32[2,64,768]{2,1,0:T(8,128)}) %all-reduce.3.cloned.1.call-update) | async-done | bytes 393232 | tf_op jit(solution)/shard_map/psum | solution.py:34
  243.9 0.0 copy-start.2
  243.9 1.7 fusion.10
  245.5 10.9 %psum.22 = f32[2,64,64]{1,2,0:T(8,128)S(1)} all-reduce(f32[2,64,64]{1,2,0:T(8,128)S(1)} %fusion.10), channel_id=1, replica_groups=mesh['dp'=8,'tensor'=4] {'tensor'}, use_global_device_ids=true, to_apply=%region_2.0 | all-reduce | flops 8192 | bytes 65536 | tf_op jit(solution)/shard_map/psum | solution.py:35
  256.4 1.9 copy.14
  258.3 0.9 gather_fusion
  259.3 0.1 multiply_add_fusion
  259.3 0.1 copy.16
  259.4 0.1 fusion.6
  259.5 11.7 %custom-call.8 = f32[2,64,64]{2,1,0:T(8,128)S(1)} custom-call(f32[2,64,64]{2,1,0:T(8,128)S(1)} %fusion.6), custom_call_target="Cholesky" | custom-call | tf_op jit(solution)/shard_map/jit(cholesky)/cholesky | solution.py:11
  271.3 0.1 compare_reduce_fusion
  271.4 0.1 select_bitcast_fusion
  271.5 9.8 %custom-call.9 = f32[2,1,64,64]{2,3,1,0:T(8,128)S(1)} custom-call(f32[2,1,64,64]{3,2,1,0:T(8,128)S(1)} %select_bitcast_fusion), custom_call_target="InvertDiagBlocksLowerTriangular" | custom-call | tf_op jit(solution)/shard_map/vmap(jit(_solve_triangular))/triangular_solve | solution.py:14
  281.3 0.0 copy-done.2
  281.3 1.3 fusion.4
  282.6 0.0 all-gather.5.cloned.1.call-update
  282.6 0.0 all-reduce.5.cloned.1.call-start
  282.7 18.8 %all-gather.5.cloned.1.call-done = f32[2,64,3072]{2,1,0:T(8,128)} async-done(((f32[2,64,768]{2,1,0:T(8,128)}), f32[2,64,3072]{2,1,0:T(8,128)}) %all-gather.5.cloned.1.call-update) | async-done | bytes 1572880 | tf_op jit(solution)/shard_map/all_gather | solution.py:37
  301.5 16.3 %convolution_convert_fusion.1 = bf16[2,64,768]{2,1,0:T(8,128)(2,1)} fusion(f32[2,64,3072]{2,1,0:T(8,128)} %all-gather.5.cloned.1.call-done, f32[2,3072,768]{2,1,0:T(8,128)} %convert_add_fusion), kind=kOutput, calls=%fused_computation.5 | convolution fusion | flops 3623976960 | bytes 20643840 | tf_op jit(solution)/shard_map/lrd,lde->lre/dot_general | solution.py:38
  317.8 0.0 all-reduce.5.cloned.1.call-update
  317.8 70.8 %all-reduce.5.cloned.1.call-done = bf16[2,64,768]{2,1,0:T(8,128)(2,1)} async-done(((bf16[2,64,768]{2,1,0:T(8,128)(2,1)}), bf16[2,64,768]{2,1,0:T(8,128)(2,1)}) %all-reduce.5.cloned.1.call-update) | async-done | bytes 196624 | tf_op jit(solution)/shard_map/psum | solution.py:39
  388.6 0.0 copy-start.3
  388.6 0.0 copy-start.1
  388.6 20.9 %subtract_convert_fusion = bf16[2,3072,768]{2,1,0:T(8,128)(2,1)} fusion(f32[2,3072,768]{2,1,0:T(8,128)} %convert_add_fusion, f32[2,64,3072]{2,1,0:T(8,128)} %all-gather.5.cloned.1.call-done, bf16[2,64,768]{2,1,0:T(8,128)(2,1)} %all-reduce.5.cloned.1.call-done), kind=kOutput, calls=%fused_computation.1 | convolution fusion | flops 3633512448 | bytes 30081024 | tf_op jit(solution)/shard_map/lrd,lre->lde/dot_general | solution.py:46
  409.5 0.0 copy-done.3
  409.5 3.1 convolution_convert_fusion
  412.6 0.0 copy-done.1
  (7 shorter events, 0.1 us)
Async XLA Ops:
  7.2 91.5 %copy-start = (bf16[2,1024,768]{2,1,0:T(8,128)(2,1)S(1)}, bf16[2,1024,768]{2,1,0:T(8,128)(2,1)}, u32[]{:S(2)}) copy-start(bf16[2,1024,768]{2,1,0:T(8,128)(2,1)} %param.4) | copy-start | bytes 9437188
  7.2 91.5 %all-gather.3.cloned.1.call-start = ((), (), s32[]{:S(2)}) async-start(), calls=%async_computation.1 | async-start | bytes 15728640 | tf_op jit(solution)/shard_map/all_gather | solution.py:27
  12.0 105.9 %copy-start.4 = (f32[2,64,768]{2,1,0:T(8,128)S(1)}, f32[2,64,768]{2,1,0:T(8,128)}, u32[]{:S(2)}) copy-start(f32[2,64,768]{2,1,0:T(8,128)} %param.7) | copy-start | bytes 1179652
  12.0 156.6 %reduce-scatter.2.cloned.1.call-start = ((), (), s32[]{:S(2)}) async-start(), calls=%async_computation.2 | async-start | bytes 1966080 | tf_op jit(solution)/shard_map/reduce_scatter | solution.py:33
  140.5 103.4 %all-reduce.3.cloned.1.call-start = ((), (), s32[]{:S(2)}) async-start(), calls=%async_computation.3 | async-start | bytes 786432 | tf_op jit(solution)/shard_map/psum | solution.py:34
  168.7 132.8 %all-gather.5.cloned.1.call-start = ((), (), s32[]{:S(2)}) async-start(), calls=%async_computation.4 | async-start | bytes 1966080 | tf_op jit(solution)/shard_map/all_gather | solution.py:37
  243.9 37.5 %copy-start.2 = (f32[2,64,768]{2,1,0:T(8,128)S(1)}, f32[2,64,768]{2,1,0:T(8,128)}, u32[]{:S(2)}) copy-start(f32[2,64,768]{2,1,0:T(8,128)} %all-reduce.3.cloned.1.call-done) | copy-start | bytes 1179652
  282.6 106.0 %all-reduce.5.cloned.1.call-start = ((), (), s32[]{:S(2)}) async-start(), calls=%async_computation.5 | async-start | bytes 393216 | tf_op jit(solution)/shard_map/psum | solution.py:39
  388.6 20.9 %copy-start.3 = (bf16[2,64,768]{2,1,0:T(8,128)(2,1)S(1)}, bf16[2,64,768]{2,1,0:T(8,128)(2,1)}, u32[]{:S(2)}) copy-start(bf16[2,64,768]{2,1,0:T(8,128)(2,1)} %all-reduce.5.cloned.1.call-done) | copy-start | bytes 589828
  388.6 24.0 %copy-start.1 = (bf16[2,1024,768]{2,1,0:T(8,128)(2,1)S(1)}, bf16[2,1024,768]{2,1,0:T(8,128)(2,1)}, u32[]{:S(2)}) copy-start(bf16[2,1024,768]{2,1,0:T(8,128)(2,1)} %param.4) | copy-start | bytes 9437188
Sparse Core Ops, SparseCore 0:
  12.2 86.4 all-gather.2
  140.6 27.9 reduce-scatter.1
  172.0 71.8 all-reduce.2
  282.8 18.6 all-gather.4
  317.9 70.6 all-reduce.4
where the time goes:
time: 419 us
  waiting for transfers between devices  279 us (67%)
  matrix products  85 us (20%)
  other arithmetic  22 us (5%)
  between operations  13.9 us (3%)
  blocking collectives  10.9 us (3%)
  local copies, waits for them, and re-layouts  7.81 us (2%)
    all_gather x1, waiting for transfers between devices, compress(): lax.all_gather(out_grad, 'tensor', axis=1, tiled=True)  86.6 us
    psum x1, waiting for transfers between devices, compress(): left_part = lax.psum(left_part, 'dp')  75 us
    psum x1, waiting for transfers between devices, compress(): lax.psum(right_terms.astype(jnp.bfloat16), 'dp').astype(jnp.float32)  70.8 us
    reduce_scatter x1, waiting for transfers between devices, compress(): lax.psum_scatter(left_factor, 'tensor', scatter_dimension=2, tiled=True)  28.1 us
    dot_general x1, matrix products, compress(): jnp.einsum('lre,lde->lrd', right_init, moment, precision=lax.Precision.HI...  22.5 us
    dot_general x1, matrix products, compress(): jnp.einsum('lrd,lre->lde', ortho_basis, right_factor / replicas, precisio...  20.9 us
    dot_general x1, matrix products, compress(): jnp.einsum('ltd,lte->lde', lax.all_gather(out_grad, 'tensor', axis=1, til...  19.3 us
    all_gather x1, waiting for transfers between devices, compress(): ortho_basis = lax.all_gather(ortho_part, 'tensor', axis=2, tiled=True)  18.8 us
  transfers between devices with their start and end apart: 5, of which 5 were waited for; matrix products, arithmetic and copies ran while one was open for 0% of the time, Pallas kernels for 0%

commit v1 on v0

--- a/solution.py
+++ b/solution.py
@@ -31,7 +31,11 @@
     moment = moment + error_in.astype(jnp.float32)
     left_factor = jnp.einsum("lre,lde->lrd", right_init, moment, precision=lax.Precision.HIGHEST)
     left_part = lax.psum_scatter(left_factor, "tensor", scatter_dimension=2, tiled=True)
-    left_part = lax.psum(left_part, "dp")
+    left_part = left_part
+    for hop in (1, 2, 4):
+        left_part = left_part + lax.ppermute(
+            left_part, "dp", [(dev, dev ^ hop) for dev in range(8)]
+        )
     gram_matrix = lax.psum(gram_of(left_part), "tensor")
     ortho_part = solve_rows(gram_matrix, left_part)
     ortho_basis = lax.all_gather(ortho_part, "tensor", axis=2, tiled=True)

time: 419 us -> 385 us (0.919)
  waiting for transfers between devices: 279 us -> 239 us
  starting transfers between devices: 0.2 us -> 5.64 us
    psum x1 -> x0, waiting for transfers between devices: 75 us -> none  [compress(): left_part = lax.psum(left_part, 'dp')]
    ppermute x0 -> x3, waiting for transfers between devices: none -> 33.6 us  [compress(): lax.ppermute(left_part, 'dp', [(dev, dev ^ hop) for dev in range(8)])]
    ppermute x0 -> x3, starting transfers between devices: none -> 5.48 us  [compress(): lax.ppermute(left_part, 'dp', [(dev, dev ^ hop) for dev in range(8)])]
  transfers between devices with their start and end apart: 5 -> 7, of which waited for: 5 -> 7; matrix products, arithmetic and copies ran while one was open for 0% -> 0% of each run, Pallas kernels for 0% -> 0%
where the time goes in v1:
time: 385 us
  waiting for transfers between devices  239 us (62%)
  matrix products  83.8 us (22%)
  other arithmetic  23.2 us (6%)
  between operations  13.9 us (4%)
  blocking collectives  11.2 us (3%)
  local copies, waits for them, and re-layouts  7.76 us (2%)
  starting transfers between devices  5.64 us (1%)
    all_gather x1, waiting for transfers between devices, compress(): lax.all_gather(out_grad, 'tensor', axis=1, tiled=True)  86.6 us
    psum x1, waiting for transfers between devices, compress(): lax.psum(right_terms.astype(jnp.bfloat16), 'dp').astype(jnp.float32)  70.8 us
    ppermute x3, waiting for transfers between devices, compress(): lax.ppermute(left_part, 'dp', [(dev, dev ^ hop) for dev in range(8)])  33.6 us
    reduce_scatter x1, waiting for transfers between devices, compress(): lax.psum_scatter(left_factor, 'tensor', scatter_dimension=2, tiled=True)  28.1 us
    dot_general x1, matrix products, compress(): jnp.einsum('lre,lde->lrd', right_init, moment, precision=lax.Precision.HI...  22.5 us
    dot_general x1, matrix products, compress(): jnp.einsum('lrd,lre->lde', ortho_basis, right_factor / replicas, precisio...  20.9 us
    all_gather x1, waiting for transfers between devices, compress(): ortho_basis = lax.all_gather(ortho_part, 'tensor', axis=2, tiled=True)  20.2 us
    dot_general x1, matrix products, compress(): jnp.einsum('ltd,lte->lde', lax.all_gather(out_grad, 'tensor', axis=1, til...  19.2 us
  transfers between devices with their start and end apart: 7, of which 7 were waited for; matrix products, arithmetic and copies ran while one was open for 0% of the time, Pallas kernels for 0%

profile of v1, /device:TPU:0, one launch (start us, length us, event | category | flops | bytes accessed | tf_op | source)
XLA Modules:
  0.0 384.8 jit_solution(5790973538068934599)
XLA Ops:
  7.2 0.0 copy-start
  7.2 0.0 all-gather.3.cloned.1.call-start
  7.2 4.8 %copy.12 = bf16[2,256,3072]{1,2,0:T(8,128)(2,1)} copy(bf16[2,256,3072]{2,1,0:T(8,128)(2,1)} %param.5) | data formatting | bytes 6291456 | tf_op args[1]
  12.0 0.0 all-gather.3.cloned.1.call-update
  12.0 0.0 copy-start.3
  12.0 0.0 reduce-scatter.2.cloned.1.call-start
  12.1 86.6 %all-gather.3.cloned.1.call-done = bf16[2,1024,3072]{1,2,0:T(8,128)(2,1)} async-done(((bf16[2,256,3072]{1,2,0:T(8,128)(2,1)}), bf16[2,1024,3072]{1,2,0:T(8,128)(2,1)}) %all-gather.3.cloned.1.call-update) | async-done | bytes 12582928 | tf_op jit(solution)/shard_map/all_gather | solution.py:27
  98.7 0.0 copy-done
  98.7 19.2 %convert_add_fusion = f32[2,3072,768]{2,1,0:T(8,128)} fusion(bf16[2,3072,768]{2,1,0:T(8,128)(2,1)} %param.6, bf16[2,1024,3072]{1,2,0:T(8,128)(2,1)} %all-gather.3.cloned.1.call-done, bf16[2,1024,768]{2,1,0:T(8,128)(2,1)S(1)} %copy-done), kind=kOutput, calls=%fused_computation.2 | convolution fusion | flops 9673113600 | bytes 44040192 | tf_op jit(solution)/shard_map/ltd,lte->lde/dot_general | solution.py:25
  117.9 0.0 copy-done.3
  117.9 22.5 %convolution_bitcast_fusion = f32[2,64,3072]{2,1,0:T(8,128)} fusion(f32[2,3072,768]{2,1,0:T(8,128)} %convert_add_fusion, f32[2,64,768]{2,1,0:T(8,128)S(1)} %copy-done.3), kind=kOutput, calls=%fused_computation.3 | convolution fusion | flops 3623878656 | bytes 20840448 | tf_op jit(solution)/shard_map/lre,lde->lrd/dot_general | solution.py:32
  140.4 0.0 reduce-scatter.2.cloned.1.call-update
  140.5 0.0 all-gather.5.cloned.1.call-start
  140.5 28.1 %reduce-scatter.2.cloned.1.call-done = f32[2,64,768]{2,1,0:T(8,128)} async-done(((f32[2,64,3072]{2,1,0:T(8,128)}), f32[2,64,768]{2,1,0:T(8,128)}) %reduce-scatter.2.cloned.1.call-update) | async-done | bytes 393232 | tf_op jit(solution)/shard_map/reduce_scatter | solution.py:33
  168.6 1.5 collective-permute-start
  170.1 9.4 %collective-permute-done = f32[2,64,768]{2,1,0:T(8,128)S(1)} collective-permute-done((f32[2,64,768]{2,1,0:T(8,128)}, f32[2,64,768]{2,1,0:T(8,128)S(1)}, u32[]{:S(2)}, u32[]{:S(2)}) %collective-permute-start) | collective-permute-done | bytes 393248 | tf_op jit(solution)/shard_map/ppermute | solution.py:36
  179.5 1.0 add.41
  180.6 1.5 collective-permute-start.1
  182.1 8.4 %collective-permute-done.1 = f32[2,64,768]{2,1,0:T(8,128)S(1)} collective-permute-done((f32[2,64,768]{2,1,0:T(8,128)S(1)}, f32[2,64,768]{2,1,0:T(8,128)S(1)}, u32[]{:S(2)}, u32[]{:S(2)}) %collective-permute-start.1) | collective-permute-done | bytes 393248 | tf_op jit(solution)/shard_map/ppermute | solution.py:36
  190.5 2.5 collective-permute-start.2
  193.0 0.1 copy.15
  193.1 15.8 %collective-permute-done.2 = f32[2,64,768]{2,1,0:T(8,128)S(1)} collective-permute-done((f32[2,64,768]{2,1,0:T(8,128)S(1)}, f32[2,64,768]{2,1,0:T(8,128)S(1)}, u32[]{:S(2)}, u32[]{:S(2)}) %collective-permute-start.2) | collective-permute-done | bytes 393248 | tf_op jit(solution)/shard_map/ppermute | solution.py:36
  208.9 0.1 add.43
  208.9 0.5 fusion.10
  209.4 11.2 %psum.14 = f32[2,64,64]{1,2,0:T(8,128)S(1)} all-reduce(f32[2,64,64]{1,2,0:T(8,128)S(1)} %fusion.10), channel_id=1, replica_groups=mesh['dp'=8,'tensor'=4] {'tensor'}, use_global_device_ids=true, to_apply=%region_1.0 | all-reduce | flops 8192 | bytes 65536 | tf_op jit(solution)/shard_map/psum | solution.py:39
  220.6 1.9 copy.14
  222.6 0.9 gather_fusion
  223.5 0.1 multiply_add_fusion
  223.6 0.1 copy.16
  223.6 0.1 fusion.6
  223.7 11.7 %custom-call.8 = f32[2,64,64]{2,1,0:T(8,128)S(1)} custom-call(f32[2,64,64]{2,1,0:T(8,128)S(1)} %fusion.6), custom_call_target="Cholesky" | custom-call | tf_op jit(solution)/shard_map/jit(cholesky)/cholesky | solution.py:11
  235.5 0.1 compare_reduce_fusion
  235.6 0.1 select_bitcast_fusion
  235.7 9.8 %custom-call.9 = f32[2,1,64,64]{2,3,1,0:T(8,128)S(1)} custom-call(f32[2,1,64,64]{3,2,1,0:T(8,128)S(1)} %select_bitcast_fusion), custom_call_target="InvertDiagBlocksLowerTriangular" | custom-call | tf_op jit(solution)/shard_map/vmap(jit(_solve_triangular))/triangular_solve | solution.py:14
  245.5 1.3 fusion.4
  246.8 0.0 all-gather.5.cloned.1.call-update
  246.8 0.0 all-reduce.2.cloned.1.call-start
  246.9 20.2 %all-gather.5.cloned.1.call-done = f32[2,64,3072]{2,1,0:T(8,128)} async-done(((f32[2,64,768]{2,1,0:T(8,128)}), f32[2,64,3072]{2,1,0:T(8,128)}) %all-gather.5.cloned.1.call-update) | async-done | bytes 1572880 | tf_op jit(solution)/shard_map/all_gather | solution.py:41
  267.1 16.3 %convolution_convert_fusion.1 = bf16[2,64,768]{2,1,0:T(8,128)(2,1)} fusion(f32[2,64,3072]{2,1,0:T(8,128)} %all-gather.5.cloned.1.call-done, f32[2,3072,768]{2,1,0:T(8,128)} %convert_add_fusion), kind=kOutput, calls=%fused_computation.5 | convolution fusion | flops 3623976960 | bytes 20643840 | tf_op jit(solution)/shard_map/lrd,lde->lre/dot_general | solution.py:42
  283.5 0.0 all-reduce.2.cloned.1.call-update
  283.5 70.8 %all-reduce.2.cloned.1.call-done = bf16[2,64,768]{2,1,0:T(8,128)(2,1)} async-done(((bf16[2,64,768]{2,1,0:T(8,128)(2,1)}), bf16[2,64,768]{2,1,0:T(8,128)(2,1)}) %all-reduce.2.cloned.1.call-update) | async-done | bytes 196624 | tf_op jit(solution)/shard_map/psum | solution.py:43
  354.3 0.0 copy-start.2
  354.3 0.0 copy-start.1
  354.3 20.9 %subtract_convert_fusion = bf16[2,3072,768]{2,1,0:T(8,128)(2,1)} fusion(f32[2,3072,768]{2,1,0:T(8,128)} %convert_add_fusion, f32[2,64,3072]{2,1,0:T(8,128)} %all-gather.5.cloned.1.call-done, bf16[2,64,768]{2,1,0:T(8,128)(2,1)} %all-reduce.2.cloned.1.call-done), kind=kOutput, calls=%fused_computation.1 | convolution fusion | flops 3633512448 | bytes 30081024 | tf_op jit(solution)/shard_map/lrd,lre->lde/dot_general | solution.py:50
  375.2 0.0 copy-done.2
  375.2 3.1 convolution_convert_fusion
  378.3 0.0 copy-done.1
  (8 shorter events, 0.1 us)
Async XLA Ops:
  7.2 91.5 %copy-start = (bf16[2,1024,768]{2,1,0:T(8,128)(2,1)S(1)}, bf16[2,1024,768]{2,1,0:T(8,128)(2,1)}, u32[]{:S(2)}) copy-start(bf16[2,1024,768]{2,1,0:T(8,128)(2,1)} %param.4) | copy-start | bytes 9437188
  7.2 91.5 %all-gather.3.cloned.1.call-start = ((), (), s32[]{:S(2)}) async-start(), calls=%async_computation.1 | async-start | bytes 15728640 | tf_op jit(solution)/shard_map/all_gather | solution.py:27
  12.0 105.9 %copy-start.3 = (f32[2,64,768]{2,1,0:T(8,128)S(1)}, f32[2,64,768]{2,1,0:T(8,128)}, u32[]{:S(2)}) copy-start(f32[2,64,768]{2,1,0:T(8,128)} %param.7) | copy-start | bytes 1179652
  12.0 156.6 %reduce-scatter.2.cloned.1.call-start = ((), (), s32[]{:S(2)}) async-start(), calls=%async_computation.2 | async-start | bytes 1966080 | tf_op jit(solution)/shard_map/reduce_scatter | solution.py:33
  140.5 126.7 %all-gather.5.cloned.1.call-start = ((), (), s32[]{:S(2)}) async-start(), calls=%async_computation.3 | async-start | bytes 1966080 | tf_op jit(solution)/shard_map/all_gather | solution.py:41
  168.6 10.9 %collective-permute-start = (f32[2,64,768]{2,1,0:T(8,128)}, f32[2,64,768]{2,1,0:T(8,128)S(1)}, u32[]{:S(2)}, u32[]{:S(2)}) collective-permute-start(f32[2,64,768]{2,1,0:T(8,128)} %reduce-scatter.2.cloned.1.call-done), channel_id=1, source_target_pairs={{0,4},{4,0},{8,12},{12,8},{16,20},{20,16},{24,28},{28,24},{1,5},{5... | collective-permute-start | bytes 1179656 | tf_op jit(solution)/shard_map/ppermute | solution.py:36
  180.6 9.9 %collective-permute-start.1 = (f32[2,64,768]{2,1,0:T(8,128)S(1)}, f32[2,64,768]{2,1,0:T(8,128)S(1)}, u32[]{:S(2)}, u32[]{:S(2)}) collective-permute-start(f32[2,64,768]{2,1,0:T(8,128)S(1)} %add.41), channel_id=1, source_target_pairs={{0,8},{4,12},{8,0},{12,4},{16,24},{20,28},{24,16},{28,20},{1,9},{5... | collective-permute-start | bytes 1179656 | tf_op jit(solution)/shard_map/ppermute | solution.py:36
  190.5 18.4 %collective-permute-start.2 = (f32[2,64,768]{2,1,0:T(8,128)S(1)}, f32[2,64,768]{2,1,0:T(8,128)S(1)}, u32[]{:S(2)}, u32[]{:S(2)}) collective-permute-start(f32[2,64,768]{2,1,0:T(8,128)S(1)} %add.42), channel_id=1, source_target_pairs={{0,16},{4,20},{8,24},{12,28},{16,0},{20,4},{24,8},{28,12},{1,17},{... | collective-permute-start | bytes 1179656 | tf_op jit(solution)/shard_map/ppermute | solution.py:36
  246.8 107.5 %all-reduce.2.cloned.1.call-start = ((), (), s32[]{:S(2)}) async-start(), calls=%async_computation.4 | async-start | bytes 393216 | tf_op jit(solution)/shard_map/psum | solution.py:43
  354.3 20.9 %copy-start.2 = (bf16[2,64,768]{2,1,0:T(8,128)(2,1)S(1)}, bf16[2,64,768]{2,1,0:T(8,128)(2,1)}, u32[]{:S(2)}) copy-start(bf16[2,64,768]{2,1,0:T(8,128)(2,1)} %all-reduce.2.cloned.1.call-done) | copy-start | bytes 589828
  354.3 24.0 %copy-start.1 = (bf16[2,1024,768]{2,1,0:T(8,128)(2,1)S(1)}, bf16[2,1024,768]{2,1,0:T(8,128)(2,1)}, u32[]{:S(2)}) copy-start(bf16[2,1024,768]{2,1,0:T(8,128)(2,1)} %param.4) | copy-start | bytes 9437188
Sparse Core Ops, SparseCore 0:
  12.2 86.4 all-gather.2
  140.6 27.9 reduce-scatter.1
  247.0 20.1 all-gather.4
  283.6 70.6 all-reduce.1
